TPU v7x, 32 devices: a whole 2x2x4 slice. The times are simulated.
32 devices in a mesh: gx: 8 (over y, x, core), gy: 4 (over z).
Axes of the slice: x: 2, y: 2, z: 4, core: 2. Of those that a mesh axis runs over, the one named last changes fastest.
Arguments:
- field: bfloat16 [64, 16, 64, 1024], P('gy', None, None, 'gx'), may hold values from -6 to 6
- conv_w: bfloat16 [27, 64, 64], replicated, may hold values from -0.15625 to 0.15625
- spec_re: float32 [16, 64, 64], replicated, may hold values from -6 to 6
- spec_im: float32 [16, 64, 64], replicated, may hold values from -6 to 6
- mlp_in: bfloat16 [256, 64], replicated, may hold values from -0.75 to 0.75
- mlp_out: bfloat16 [64, 256], replicated, may hold values from -0.375 to 0.375
Outputs:
- result: bfloat16 [64, 16, 64, 1024], P('gy', None, None, 'gx')
All inputs are finite; a program needn't handle non-finite values.
Results may differ from a plain program's by a relative error of at most 0.0062.
Values may be sent and summed in bfloat16 or wider, within the bound.
A program may use at most 128 MiB of HBM per device.

v0:
```python
import functools
import math

import jax
import jax.numpy as jnp
from jax import lax
from jax.experimental import pallas as pl
from jax.experimental.pallas import tpu as pltpu
from jax.sharding import PartitionSpec as P

F32 = jnp.float32
BF16 = jnp.bfloat16
MESH = pl.DeviceIdType.MESH
CHUNKS = 4
NT = (((1,), (1,)), ((), ()))
TN = (((0,), (0,)), ((), ()))


def kernel(
    n, m, field, conv_w, spec_re, spec_im, mlp_in, mlp_out, out,
    xs, lifted, halo_out, halo_in, halo_top, halo_bot, toep, mixw, fwd, inv,
    part, got, tsum, mixed,
    load_sem, store_sem, row_send, row_recv, side_send, side_recv, corner_send, corner_recv,
    rs_send, rs_recv, ag_send, ag_recv,
):
    rows, depth, ch, width = field.shape
    modes = spec_re.shape[0]
    total = n * width
    pairs = depth // 2
    crows = rows // CHUNKS
    cpairs = crows * pairs
    share = cpairs // n
    per = width // depth
    groups = rows // per
    me = lax.axis_index("gx")
    my = lax.axis_index("gy")
    has_left, has_right = me > 0, me < n - 1
    has_up, has_down = my > 0, my < m - 1

    def load(y):
        return pltpu.make_async_copy(
            field.at[y], xs.at[1, y + 1, pl.ds(1, depth)], load_sem.at[y]
        )

    @pl.loop(0, rows)
    def _(y):
        load(y).start()

    barrier = pltpu.get_barrier_semaphore()

    @pl.loop(1, n)
    def _(o):
        pl.semaphore_signal(
            barrier, inc=1, device_id={"gx": lax.rem(me + o, n)}, device_id_type=MESH
        )

    @pl.when(has_up)
    def _():
        pl.semaphore_signal(barrier, inc=1, device_id={"gy": my - 1}, device_id_type=MESH)

    @pl.when(has_down)
    def _():
        pl.semaphore_signal(barrier, inc=1, device_id={"gy": my + 1}, device_id_type=MESH)

    pl.semaphore_wait(barrier, n - 1 + has_up.astype(jnp.int32) + has_down.astype(jnp.int32))

    def row_up():
        return pltpu.make_async_remote_copy(
            src_ref=field.at[0], dst_ref=xs.at[1, rows + 1, pl.ds(1, depth)],
            send_sem=row_send.at[0], recv_sem=row_recv.at[0],
            device_id={"gy": my - 1}, device_id_type=MESH,
        )

    def row_down():
        return pltpu.make_async_remote_copy(
            src_ref=field.at[rows - 1], dst_ref=xs.at[1, 0, pl.ds(1, depth)],
            send_sem=row_send.at[1], recv_sem=row_recv.at[1],
            device_id={"gy": my + 1}, device_id_type=MESH,
        )

    pl.when(has_up)(lambda: row_up().start())
    pl.when(has_down)(lambda: row_down().start())

    lane = lax.broadcasted_iota(jnp.int32, (ch, width), 1)

    for g in range(groups):
        for y in range(g * per, (g + 1) * per):
            load(y).wait()
        first = jnp.zeros((ch, width), BF16)
        last = jnp.zeros((ch, width), BF16)
        for y in range(per):
            for z in range(depth):
                tile = xs[1, g * per + y + 1, z + 1]
                to = y * depth + z
                first = jnp.where(lane == to, tile if to == 0 else pltpu.roll(tile, to, 1), first)
                back = (to + 1) % width
                last = jnp.where(lane == to, tile if back == 0 else pltpu.roll(tile, back, 1), last)
        halo_out[0, g] = first
        halo_out[1, g] = last

    def side_left(g):
        return pltpu.make_async_remote_copy(
            src_ref=halo_out.at[0, g], dst_ref=halo_in.at[g, 1],
            send_sem=side_send.at[0, g], recv_sem=side_recv.at[1, g],
            device_id={"gx": me - 1}, device_id_type=MESH,
        )

    def side_right(g):
        return pltpu.make_async_remote_copy(
            src_ref=halo_out.at[1, g], dst_ref=halo_in.at[g, 0],
            send_sem=side_send.at[1, g], recv_sem=side_recv.at[0, g],
            device_id={"gx": me + 1}, device_id_type=MESH,
        )

    for g in range(groups):
        pl.when(has_left)(lambda g=g: side_left(g).start())
        pl.when(has_right)(lambda g=g: side_right(g).start())

    blank = jnp.zeros((ch, width), BF16)

    @pl.loop(0, rows + 2)
    def _(y):
        for d in range(3):
            xs[d, y, 0] = blank
            xs[d, y, depth + 1] = blank

    @pl.when(jnp.logical_not(has_up))
    def _():
        for z in range(depth):
            xs[1, 0, z + 1] = blank
        for s in range(2):
            halo_top[s] = blank

    @pl.when(jnp.logical_not(has_down))
    def _():
        for z in range(depth):
            xs[1, rows + 1, z + 1] = blank
        for s in range(2):
            halo_bot[s] = blank

    @pl.when(jnp.logical_not(has_left))
    def _():
        for g in range(groups):
            halo_in[g, 0] = blank

    @pl.when(jnp.logical_not(has_right))
    def _():
        for g in range(groups):
            halo_in[g, 1] = blank

    square = jnp.zeros((ch, ch), BF16)
    for a in range(3):
        for d in range(3):
            t = a * 3 + d
            taps = [conv_w[(a * 3 + b) * 3 + d] for b in range(3)]
            cols = pl.ds(t * 4 * ch, 4 * ch)
            toep[0:ch, cols] = jnp.concatenate(taps + [square], axis=1)
            toep[ch:2 * ch, cols] = jnp.concatenate([square] + taps, axis=1)

    @pl.loop(0, modes)
    def _(k):
        re = spec_re[k].astype(BF16)
        im = spec_im[k].astype(BF16)
        neg = -im
        mixw[k, 0:ch] = jnp.concatenate([re, square, neg, square], axis=1)
        mixw[k, ch:2 * ch] = jnp.concatenate([square, re, square, neg], axis=1)
        mixw[k, 2 * ch:3 * ch] = jnp.concatenate([im, square, re, square], axis=1)
        mixw[k, 3 * ch:4 * ch] = jnp.concatenate([square, im, square, re], axis=1)

    places = me * width + lax.broadcasted_iota(jnp.int32, (modes, width), 1)
    orders = lax.broadcasted_iota(jnp.int32, (modes, width), 0)
    angle = lax.rem(places * orders, total).astype(F32) * (2.0 * math.pi / total)
    cosine, sine = jnp.cos(angle), -jnp.sin(angle)
    fwd[...] = jnp.concatenate([cosine, sine], axis=0).astype(BF16)
    scales = jnp.where(orders == 0, 1.0, 2.0).astype(F32) / total
    table = jnp.concatenate([cosine * scales, sine * scales], axis=0)
    high = table.astype(BF16)
    inv[0:2 * modes] = high
    inv[2 * modes:4 * modes] = (table - high.astype(F32)).astype(BF16)

    for g in range(groups):
        pl.when(has_left)(lambda g=g: side_right(g).wait_recv())
        pl.when(has_right)(lambda g=g: side_left(g).wait_recv())

    def corner_up():
        return pltpu.make_async_remote_copy(
            src_ref=halo_in.at[0], dst_ref=halo_bot,
            send_sem=corner_send.at[0], recv_sem=corner_recv.at[0],
            device_id={"gy": my - 1}, device_id_type=MESH,
        )

    def corner_down():
        return pltpu.make_async_remote_copy(
            src_ref=halo_in.at[groups - 1], dst_ref=halo_top,
            send_sem=corner_send.at[1], recv_sem=corner_recv.at[1],
            device_id={"gy": my + 1}, device_id_type=MESH,
        )

    pl.when(has_up)(lambda: corner_up().start())
    pl.when(has_down)(lambda: corner_down().start())

    def shift_row(y, left, right):
        for z in range(depth):
            tile = xs[1, y, z + 1]
            edge = left if z == 0 else pltpu.roll(left, width - z, 1)
            xs[0, y, z + 1] = jnp.where(lane == 0, edge, pltpu.roll(tile, 1, 1))
            xs[2, y, z + 1] = jnp.where(
                lane == width - 1,
                pltpu.roll(right, width - 1 - z, 1),
                pltpu.roll(tile, width - 1, 1),
            )

    def shift_own(y):
        g = y // per
        turn = lax.rem(width - lax.rem(y, per) * depth, width)
        shift_row(y + 1, pltpu.roll(halo_in[g, 0], turn, 1), pltpu.roll(halo_in[g, 1], turn, 1))

    def lift_row(y):
        for q in range(depth // 4):
            blocks = []
            for a in range(3):
                for d in range(3):
                    one = xs[d, y + a, pl.ds(4 * q, 4)].reshape(4 * ch, width)
                    two = xs[d, y + a, pl.ds(4 * q + 2, 4)].reshape(4 * ch, width)
                    blocks.append(jnp.concatenate([one, two], axis=1))
            acc = jnp.dot(toep[...], jnp.concatenate(blocks, axis=0), preferred_element_type=F32)
            for p in range(2):
                own = xs[1, y + 1, pl.ds(4 * q + 2 * p + 1, 2)].reshape(2 * ch, width)
                new = (own.astype(F32) + acc[:, p * width:(p + 1) * width]).astype(BF16)
                lifted[y, 2 * q + p] = new
                modes_part = lax.dot_general(fwd[...], new, NT, preferred_element_type=F32)
                part[y * pairs + 2 * q + p] = modes_part.astype(BF16)

    def rs_copy(c, o):
        to = lax.rem(me + o, n)
        return pltpu.make_async_remote_copy(
            src_ref=part.at[pl.ds(c * cpairs + to * share, share)], dst_ref=got.at[c, o],
            send_sem=rs_send.at[c, o], recv_sem=rs_recv.at[c, o],
            device_id={"gx": to}, device_id_type=MESH,
        )

    def ag_copy(c, o):
        mine = pl.ds(c * cpairs + me * share, share)
        return pltpu.make_async_remote_copy(
            src_ref=mixed.at[mine], dst_ref=mixed.at[mine],
            send_sem=ag_send.at[c, o], recv_sem=ag_recv.at[c, o],
            device_id={"gx": lax.rem(me + o, n)}, device_id_type=MESH,
        )

    def ag_wait(c, o):
        theirs = pl.ds(c * cpairs + lax.rem(me + n - o, n) * share, share)
        pltpu.make_async_remote_copy(
            src_ref=mixed.at[theirs], dst_ref=mixed.at[theirs],
            send_sem=ag_send.at[c, o], recv_sem=ag_recv.at[c, o],
            device_id={"gx": lax.rem(me + o, n)}, device_id_type=MESH,
        ).wait_recv()

    def lift_chunk(c):
        pl.loop(c * crows, (c + 1) * crows)(lift_row)
        pl.loop(1, n)(lambda o: rs_copy(c, o).start())

    def mix_chunk(c):
        mine = pl.ds(c * cpairs + me * share, share)
        tsum[...] = part[mine].astype(F32)

        @pl.loop(1, n)
        def _(o):
            rs_copy(c, o).wait_recv()
            tsum[...] += got[c, o].astype(F32)

        for k in range(modes):
            data = jnp.concatenate([tsum[:, k, :], tsum[:, modes + k, :]], axis=1)
            top = data.astype(BF16).astype(F32)
            lhs = jnp.concatenate([top, data - top], axis=0).astype(BF16)
            both = lax.dot_general(lhs, mixw[k], NT, preferred_element_type=F32)
            new = both[0:share] + both[share:2 * share]
            tsum[:, k, :] = new[:, :width]
            tsum[:, modes + k, :] = new[:, width:]
        mixed[mine] = tsum[...].astype(BF16)
        pl.loop(1, n)(lambda o: ag_copy(c, o).start())

    def store(y):
        return pltpu.make_async_copy(lifted.at[y], out.at[y], store_sem.at[y])

    slope = math.sqrt(2.0 / math.pi)

    def finish_row(y):
        for p in range(pairs):
            spec = mixed[y * pairs + p]
            branch = lax.dot_general(
                jnp.concatenate([spec, spec], axis=0), inv[...], TN, preferred_element_type=F32
            )
            blended = (lifted[y, p].astype(F32) + branch).astype(BF16)
            wide = jnp.concatenate([blended[0:ch], blended[ch:2 * ch]], axis=1)
            h = jnp.dot(mlp_in[...], wide, preferred_element_type=F32)
            h = h * (0.5 + 0.5 * jnp.tanh(h * (slope + (slope * 0.044715) * (h * h))))
            down = jnp.dot(mlp_out[...], h.astype(BF16), preferred_element_type=F32)
            res = (wide.astype(F32) + down).astype(BF16)
            lifted[y, p] = jnp.concatenate([res[:, :width], res[:, width:]], axis=0)
        store(y).start()

    def finish_chunk(c):
        pl.loop(1, n)(lambda o: ag_wait(c, o))
        pl.loop(c * crows, (c + 1) * crows)(finish_row)

    pl.loop(0, rows)(shift_own)
    inner = list(range(1, CHUNKS - 1))
    for c in inner:
        lift_chunk(c)
    mix_chunk(inner[0])

    pl.when(has_up)(lambda: row_down().wait_recv())
    pl.when(has_up)(lambda: corner_down().wait_recv())
    turn = width - (per - 1) * depth
    shift_row(0, pltpu.roll(halo_top[0], turn, 1), pltpu.roll(halo_top[1], turn, 1))
    lift_chunk(0)
    for c in inner[1:]:
        mix_chunk(c)
    pl.when(has_down)(lambda: row_up().wait_recv())
    pl.when(has_down)(lambda: corner_up().wait_recv())
    shift_row(rows + 1, halo_bot[0], halo_bot[1])
    lift_chunk(CHUNKS - 1)
    mix_chunk(0)
    finish_chunk(inner[0])
    mix_chunk(CHUNKS - 1)
    for c in inner[1:] + [0, CHUNKS - 1]:
        finish_chunk(c)

    pl.loop(0, rows)(lambda y: store(y).wait())
    pl.when(has_up)(lambda: row_up().wait_send())
    pl.when(has_down)(lambda: row_down().wait_send())
    pl.when(has_up)(lambda: corner_up().wait_send())
    pl.when(has_down)(lambda: corner_down().wait_send())
    for g in range(groups):
        pl.when(has_left)(lambda g=g: side_left(g).wait_send())
        pl.when(has_right)(lambda g=g: side_right(g).wait_send())
    for c in range(CHUNKS):
        @pl.loop(1, n)
        def _(o):
            rs_copy(c, o).wait_send()
            ag_copy(c, o).wait_send()


def per_device(n, m, field, conv_w, spec_re, spec_im, mlp_in, mlp_out):
    rows, depth, ch, width = field.shape
    modes = spec_re.shape[0]
    pairs = depth // 2
    cpairs = rows // CHUNKS * pairs
    share = cpairs // n
    groups = rows * depth // width
    dma = pltpu.SemaphoreType.DMA
    vmem = pl.BlockSpec(memory_space=pltpu.VMEM)
    result = pl.pallas_call(
        functools.partial(kernel, n, m),
        out_shape=jax.ShapeDtypeStruct((rows, pairs, 2 * ch, width), BF16),
        in_specs=[pl.BlockSpec(memory_space=pl.ANY)] + [vmem] * 5,
        out_specs=pl.BlockSpec(memory_space=pl.ANY),
        scratch_shapes=[
            pltpu.VMEM((3, rows + 2, depth + 2, ch, width), BF16),
            pltpu.VMEM((rows, pairs, 2 * ch, width), BF16),
            pltpu.VMEM((2, groups, ch, width), BF16),
            pltpu.VMEM((groups, 2, ch, width), BF16),
            pltpu.VMEM((2, ch, width), BF16),
            pltpu.VMEM((2, ch, width), BF16),
            pltpu.VMEM((2 * ch, 36 * ch), BF16),
            pltpu.VMEM((modes, 4 * ch, 4 * ch), BF16),
            pltpu.VMEM((2 * modes, width), BF16),
            pltpu.VMEM((4 * modes, width), BF16),
            pltpu.VMEM((rows * pairs, 2 * modes, width), BF16),
            pltpu.VMEM((CHUNKS, n, share, 2 * modes, width), BF16),
            pltpu.VMEM((share, 2 * modes, width), F32),
            pltpu.VMEM((rows * pairs, 2 * modes, width), BF16),
            dma((rows,)), dma((rows,)),
            dma((2,)), dma((2,)),
            dma((2, groups)), dma((2, groups)),
            dma((2,)), dma((2,)),
            dma((CHUNKS, n)), dma((CHUNKS, n)),
            dma((CHUNKS, n)), dma((CHUNKS, n)),
        ],
        compiler_params=pltpu.CompilerParams(
            collective_id=0, has_side_effects=True, vmem_limit_bytes=56 << 20
        ),
    )(field, conv_w, spec_re, spec_im, mlp_in, mlp_out)
    return result.reshape(rows, depth, ch, width)


def solution(mesh):
    in_specs = (P("gy", None, None, "gx"), P(), P(), P(), P(), P())
    out_specs = P("gy", None, None, "gx")
    return jax.shard_map(
        functools.partial(per_device, mesh.shape["gx"], mesh.shape["gy"]),
        mesh=mesh, in_specs=in_specs, out_specs=out_specs, check_vma=False,
    )
```

profile of v0, /device:TPU:1, one launch (start us, length us, event | category | flops | bytes accessed | tf_op | source)
XLA Modules:
  0.0 107.9 jit_solution(16612493867708188832)
XLA Ops:
  0.0 1.5 %copy.7.mlp_in = bf16[256,64]{1,0:T(8,128)(2,1)} copy(bf16[256,64]{0,1:T(8,128)(2,1)} %param.10) | data formatting | bytes 65536 | tf_op args[4]
  1.5 100.9 %shard_map.64 = bf16[16,8,128,128]{3,2,1,0:T(8,128)(2,1)} custom-call(bf16[16,16,64,128]{3,2,1,0:T(8,128)(2,1)} %field.1, bf16[27,64,64]{2,1,0:T(8,128)(2,1)} %conv_w.1, f32[16,64,64]{2,1,0:T(8,128)} %spec_re.1, f32[16,64,64]{2,1,0:T(8,128)} %spec_im.1, bf16[256,64]{1,0:T(8,128)(2,1)} %copy.7.mlp_in, bf16[64,256]{1,0:T(8,128)(2,1)} %mlp_out.1), custom_call_target="tpu_custom_call" | custom-call | tf_op jit(solution)/shard_map/pallas_call | solution.py:353
  102.4 5.5 %copy.9 = bf16[16,16,64,128]{3,2,1,0:T(8,128)(2,1)} copy(bf16[16,16,64,128]{3,2,1,0:T(8,128)(2,1)} %bitcast.1) | data formatting | bytes 8388608
where the time goes:
time: 108 us
  Pallas kernels  101 us (94%)
  local copies, waits for them, and re-layouts  7.01 us (6%)
    pallas_call x1, Pallas kernels, per_device(): pl.pallas_call(functools.partial(kernel, n, m), out_shape=jax.ShapeDtypeS...  101 us
    unnamed x2, local copies, waits for them, and re-layouts  7.01 us

commit v1 on v0

--- a/solution.py
+++ b/solution.py
@@ -18,9 +18,9 @@
 
 def kernel(
     n, m, field, conv_w, spec_re, spec_im, mlp_in, mlp_out, out,
-    xs, lifted, halo_out, halo_in, halo_top, halo_bot, toep, mixw, fwd, inv,
+    xs, shifted, carry_a, carry_b, lifted, halo_out, halo_in, up_w, down_w, toep, mixw, fwd, inv,
     part, got, tsum, mixed,
-    load_sem, store_sem, row_send, row_recv, side_send, side_recv, corner_send, corner_recv,
+    load_sem, row_send, row_recv, side_send, side_recv, corner_send, corner_recv,
     rs_send, rs_recv, ag_send, ag_recv,
 ):
     rows, depth, ch, width = field.shape
@@ -39,7 +39,7 @@
 
     def load(y):
         return pltpu.make_async_copy(
-            field.at[y], xs.at[1, y + 1, pl.ds(1, depth)], load_sem.at[y]
+            field.at[y], xs.at[y + 1, pl.ds(1, depth)], load_sem.at[y]
         )
 
     @pl.loop(0, rows)
@@ -66,14 +66,14 @@
 
     def row_up():
         return pltpu.make_async_remote_copy(
-            src_ref=field.at[0], dst_ref=xs.at[1, rows + 1, pl.ds(1, depth)],
+            src_ref=field.at[0], dst_ref=xs.at[rows + 1, pl.ds(1, depth)],
             send_sem=row_send.at[0], recv_sem=row_recv.at[0],
             device_id={"gy": my - 1}, device_id_type=MESH,
         )
 
     def row_down():
         return pltpu.make_async_remote_copy(
-            src_ref=field.at[rows - 1], dst_ref=xs.at[1, 0, pl.ds(1, depth)],
+            src_ref=field.at[rows - 1], dst_ref=xs.at[0, pl.ds(1, depth)],
             send_sem=row_send.at[1], recv_sem=row_recv.at[1],
             device_id={"gy": my + 1}, device_id_type=MESH,
         )
@@ -90,7 +90,7 @@
         last = jnp.zeros((ch, width), BF16)
         for y in range(per):
             for z in range(depth):
-                tile = xs[1, g * per + y + 1, z + 1]
+                tile = xs[g * per + y + 1, z + 1]
                 to = y * depth + z
                 first = jnp.where(lane == to, tile if to == 0 else pltpu.roll(tile, to, 1), first)
                 back = (to + 1) % width
@@ -100,14 +100,14 @@
 
     def side_left(g):
         return pltpu.make_async_remote_copy(
-            src_ref=halo_out.at[0, g], dst_ref=halo_in.at[g, 1],
+            src_ref=halo_out.at[0, g], dst_ref=halo_in.at[g + 1, 1],
             send_sem=side_send.at[0, g], recv_sem=side_recv.at[1, g],
             device_id={"gx": me - 1}, device_id_type=MESH,
         )
 
     def side_right(g):
         return pltpu.make_async_remote_copy(
-            src_ref=halo_out.at[1, g], dst_ref=halo_in.at[g, 0],
+            src_ref=halo_out.at[1, g], dst_ref=halo_in.at[g + 1, 0],
             send_sem=side_send.at[1, g], recv_sem=side_recv.at[0, g],
             device_id={"gx": me + 1}, device_id_type=MESH,
         )
@@ -120,42 +120,47 @@
 
     @pl.loop(0, rows + 2)
     def _(y):
-        for d in range(3):
-            xs[d, y, 0] = blank
-            xs[d, y, depth + 1] = blank
+        xs[y, 0] = blank
+        xs[y, depth + 1] = blank
+
+    for d in range(2):
+        shifted[d, 0] = blank
+        shifted[d, depth + 1] = blank
 
     @pl.when(jnp.logical_not(has_up))
     def _():
         for z in range(depth):
-            xs[1, 0, z + 1] = blank
+            xs[0, z + 1] = blank
         for s in range(2):
-            halo_top[s] = blank
+            halo_in[0, s] = blank
 
     @pl.when(jnp.logical_not(has_down))
     def _():
         for z in range(depth):
-            xs[1, rows + 1, z + 1] = blank
+            xs[rows + 1, z + 1] = blank
         for s in range(2):
-            halo_bot[s] = blank
+            halo_in[groups + 1, s] = blank
 
     @pl.when(jnp.logical_not(has_left))
     def _():
         for g in range(groups):
-            halo_in[g, 0] = blank
+            halo_in[g + 1, 0] = blank
 
     @pl.when(jnp.logical_not(has_right))
     def _():
         for g in range(groups):
-            halo_in[g, 1] = blank
+            halo_in[g + 1, 1] = blank
+
+    up_w[...] = mlp_in[...].astype(F32).T.astype(BF16)
+    down_w[...] = mlp_out[...] * jnp.asarray(0.5, BF16)
 
     square = jnp.zeros((ch, ch), BF16)
     for a in range(3):
         for d in range(3):
-            t = a * 3 + d
             taps = [conv_w[(a * 3 + b) * 3 + d] for b in range(3)]
-            cols = pl.ds(t * 4 * ch, 4 * ch)
-            toep[0:ch, cols] = jnp.concatenate(taps + [square], axis=1)
-            toep[ch:2 * ch, cols] = jnp.concatenate([square] + taps, axis=1)
+            cols = pl.ds(d * 4 * ch, 4 * ch)
+            toep[pl.ds(2 * a * ch, ch), cols] = jnp.concatenate(taps + [square], axis=1)
+            toep[pl.ds((2 * a + 1) * ch, ch), cols] = jnp.concatenate([square] + taps, axis=1)
 
     @pl.loop(0, modes)
     def _(k):
@@ -184,14 +189,14 @@
 
     def corner_up():
         return pltpu.make_async_remote_copy(
-            src_ref=halo_in.at[0], dst_ref=halo_bot,
+            src_ref=halo_in.at[1], dst_ref=halo_in.at[groups + 1],
             send_sem=corner_send.at[0], recv_sem=corner_recv.at[0],
             device_id={"gy": my - 1}, device_id_type=MESH,
         )
 
     def corner_down():
         return pltpu.make_async_remote_copy(
-            src_ref=halo_in.at[groups - 1], dst_ref=halo_top,
+            src_ref=halo_in.at[groups], dst_ref=halo_in.at[0],
             send_sem=corner_send.at[1], recv_sem=corner_recv.at[1],
             device_id={"gy": my + 1}, device_id_type=MESH,
         )
@@ -199,37 +204,49 @@
     pl.when(has_up)(lambda: corner_up().start())
     pl.when(has_down)(lambda: corner_down().start())
 
-    def shift_row(y, left, right):
+    def shift_row(i):
+        g = (i - 1 + per) // per
+        turn = lax.rem(width - lax.rem(i - 1 + per, per) * depth, width)
+        left = pltpu.roll(halo_in[g, 0], turn, 1)
+        right = pltpu.roll(halo_in[g, 1], turn, 1)
         for z in range(depth):
-            tile = xs[1, y, z + 1]
+            tile = xs[i, z + 1]
             edge = left if z == 0 else pltpu.roll(left, width - z, 1)
-            xs[0, y, z + 1] = jnp.where(lane == 0, edge, pltpu.roll(tile, 1, 1))
-            xs[2, y, z + 1] = jnp.where(
+            shifted[0, z + 1] = jnp.where(lane == 0, edge, pltpu.roll(tile, 1, 1))
+            shifted[1, z + 1] = jnp.where(
                 lane == width - 1,
                 pltpu.roll(right, width - 1 - z, 1),
                 pltpu.roll(tile, width - 1, 1),
             )
 
-    def shift_own(y):
-        g = y // per
-        turn = lax.rem(width - lax.rem(y, per) * depth, width)
-        shift_row(y + 1, pltpu.roll(halo_in[g, 0], turn, 1), pltpu.roll(halo_in[g, 1], turn, 1))
-
-    def lift_row(y):
+    def window(i, d, z):
+        at = pl.ds(z, 4)
+        tile = xs[i, at] if d == 1 else shifted[d // 2, at]
+        return tile.reshape(4 * ch, width)
+
+    def lift_row(i, taps=3):
+        shift_row(i)
         for q in range(depth // 4):
-            blocks = []
-            for a in range(3):
-                for d in range(3):
-                    one = xs[d, y + a, pl.ds(4 * q, 4)].reshape(4 * ch, width)
-                    two = xs[d, y + a, pl.ds(4 * q + 2, 4)].reshape(4 * ch, width)
-                    blocks.append(jnp.concatenate([one, two], axis=1))
-            acc = jnp.dot(toep[...], jnp.concatenate(blocks, axis=0), preferred_element_type=F32)
-            for p in range(2):
-                own = xs[1, y + 1, pl.ds(4 * q + 2 * p + 1, 2)].reshape(2 * ch, width)
-                new = (own.astype(F32) + acc[:, p * width:(p + 1) * width]).astype(BF16)
-                lifted[y, 2 * q + p] = new
-                modes_part = lax.dot_general(fwd[...], new, NT, preferred_element_type=F32)
-                part[y * pairs + 2 * q + p] = modes_part.astype(BF16)
+            rhs = jnp.concatenate(
+                [
+                    jnp.concatenate([window(i, d, 4 * q), window(i, d, 4 * q + 2)], axis=1)
+                    for d in range(3)
+                ],
+                axis=0,
+            )
+            acc = jnp.dot(toep[0:2 * ch * taps], rhs, preferred_element_type=F32)
+            if taps == 3:
+                y = i - 2
+                done = carry_b[q] + acc[4 * ch:6 * ch]
+                for p in range(2):
+                    own = xs[y + 1, pl.ds(4 * q + 2 * p + 1, 2)].reshape(2 * ch, width)
+                    new = (own.astype(F32) + done[:, p * width:(p + 1) * width]).astype(BF16)
+                    lifted[y, 2 * q + p] = new
+                    modes_part = lax.dot_general(fwd[...], new, NT, preferred_element_type=F32)
+                    part[y * pairs + 2 * q + p] = modes_part.astype(BF16)
+            if taps >= 2:
+                carry_b[q] = carry_a[q] + acc[2 * ch:4 * ch]
+            carry_a[q] = acc[0:2 * ch]
 
     def rs_copy(c, o):
         to = lax.rem(me + o, n)
@@ -256,7 +273,7 @@
         ).wait_recv()
 
     def lift_chunk(c):
-        pl.loop(c * crows, (c + 1) * crows)(lift_row)
+        pl.loop(c * crows + 2, (c + 1) * crows + 2)(lift_row)
         pl.loop(1, n)(lambda o: rs_copy(c, o).start())
 
     def mix_chunk(c):
@@ -279,10 +296,9 @@
         mixed[mine] = tsum[...].astype(BF16)
         pl.loop(1, n)(lambda o: ag_copy(c, o).start())
 
-    def store(y):
-        return pltpu.make_async_copy(lifted.at[y], out.at[y], store_sem.at[y])
-
     slope = math.sqrt(2.0 / math.pi)
+    low = jnp.asarray(slope, BF16)
+    cubic = jnp.asarray(slope * 0.044715, BF16)
 
     def finish_row(y):
         for p in range(pairs):
@@ -292,41 +308,34 @@
             )
             blended = (lifted[y, p].astype(F32) + branch).astype(BF16)
             wide = jnp.concatenate([blended[0:ch], blended[ch:2 * ch]], axis=1)
-            h = jnp.dot(mlp_in[...], wide, preferred_element_type=F32)
-            h = h * (0.5 + 0.5 * jnp.tanh(h * (slope + (slope * 0.044715) * (h * h))))
-            down = jnp.dot(mlp_out[...], h.astype(BF16), preferred_element_type=F32)
+            h = jnp.dot(up_w[...], wide, preferred_element_type=F32).astype(BF16)
+            t = jnp.tanh(h * (low + cubic * (h * h)))
+            down = jnp.dot(down_w[...], h + h * t, preferred_element_type=F32)
             res = (wide.astype(F32) + down).astype(BF16)
-            lifted[y, p] = jnp.concatenate([res[:, :width], res[:, width:]], axis=0)
-        store(y).start()
+            out[y, p, 0:ch] = res[:, :width]
+            out[y, p, ch:2 * ch] = res[:, width:]
 
     def finish_chunk(c):
         pl.loop(1, n)(lambda o: ag_wait(c, o))
         pl.loop(c * crows, (c + 1) * crows)(finish_row)
 
-    pl.loop(0, rows)(shift_own)
-    inner = list(range(1, CHUNKS - 1))
-    for c in inner:
-        lift_chunk(c)
-    mix_chunk(inner[0])
-
     pl.when(has_up)(lambda: row_down().wait_recv())
     pl.when(has_up)(lambda: corner_down().wait_recv())
-    turn = width - (per - 1) * depth
-    shift_row(0, pltpu.roll(halo_top[0], turn, 1), pltpu.roll(halo_top[1], turn, 1))
-    lift_chunk(0)
-    for c in inner[1:]:
-        mix_chunk(c)
+    lift_row(0, 1)
+    lift_row(1, 2)
+    for c in range(CHUNKS - 1):
+        lift_chunk(c)
+        if c:
+            mix_chunk(c - 1)
     pl.when(has_down)(lambda: row_up().wait_recv())
     pl.when(has_down)(lambda: corner_up().wait_recv())
-    shift_row(rows + 1, halo_bot[0], halo_bot[1])
     lift_chunk(CHUNKS - 1)
-    mix_chunk(0)
-    finish_chunk(inner[0])
+    mix_chunk(CHUNKS - 2)
+    finish_chunk(0)
     mix_chunk(CHUNKS - 1)
-    for c in inner[1:] + [0, CHUNKS - 1]:
+    for c in range(1, CHUNKS):
         finish_chunk(c)
 
-    pl.loop(0, rows)(lambda y: store(y).wait())
     pl.when(has_up)(lambda: row_up().wait_send())
     pl.when(has_down)(lambda: row_down().wait_send())
     pl.when(has_up)(lambda: corner_up().wait_send())
@@ -352,17 +361,20 @@
     vmem = pl.BlockSpec(memory_space=pltpu.VMEM)
     result = pl.pallas_call(
         functools.partial(kernel, n, m),
-        out_shape=jax.ShapeDtypeStruct((rows, pairs, 2 * ch, width), BF16),
-        in_specs=[pl.BlockSpec(memory_space=pl.ANY)] + [vmem] * 5,
-        out_specs=pl.BlockSpec(memory_space=pl.ANY),
+        out_shape=pltpu.VMEM((rows, pairs, 2 * ch, width), BF16),
+        in_specs=[pl.BlockSpec(memory_space=pltpu.HBM)] + [vmem] * 5,
+        out_specs=vmem,
         scratch_shapes=[
-            pltpu.VMEM((3, rows + 2, depth + 2, ch, width), BF16),
+            pltpu.VMEM((rows + 2, depth + 2, ch, width), BF16),
+            pltpu.VMEM((2, depth + 2, ch, width), BF16),
+            pltpu.VMEM((depth // 4, 2 * ch, 2 * width), F32),
+            pltpu.VMEM((depth // 4, 2 * ch, 2 * width), F32),
             pltpu.VMEM((rows, pairs, 2 * ch, width), BF16),
             pltpu.VMEM((2, groups, ch, width), BF16),
-            pltpu.VMEM((groups, 2, ch, width), BF16),
-            pltpu.VMEM((2, ch, width), BF16),
-            pltpu.VMEM((2, ch, width), BF16),
-            pltpu.VMEM((2 * ch, 36 * ch), BF16),
+            pltpu.VMEM((groups + 2, 2, ch, width), BF16),
+            pltpu.VMEM(mlp_in.shape, BF16),
+            pltpu.VMEM(mlp_out.shape, BF16),
+            pltpu.VMEM((6 * ch, 12 * ch), BF16),
             pltpu.VMEM((modes, 4 * ch, 4 * ch), BF16),
             pltpu.VMEM((2 * modes, width), BF16),
             pltpu.VMEM((4 * modes, width), BF16),
@@ -370,7 +382,7 @@
             pltpu.VMEM((CHUNKS, n, share, 2 * modes, width), BF16),
             pltpu.VMEM((share, 2 * modes, width), F32),
             pltpu.VMEM((rows * pairs, 2 * modes, width), BF16),
-            dma((rows,)), dma((rows,)),
+            dma((rows,)),
             dma((2,)), dma((2,)),
             dma((2, groups)), dma((2, groups)),
             dma((2,)), dma((2,)),
@@ -378,9 +390,9 @@
             dma((CHUNKS, n)), dma((CHUNKS, n)),
         ],
         compiler_params=pltpu.CompilerParams(
-            collective_id=0, has_side_effects=True, vmem_limit_bytes=56 << 20
+            collective_id=0, has_side_effects=True, vmem_limit_bytes=40 << 20
         ),
-    )(field, conv_w, spec_re, spec_im, mlp_in, mlp_out)
+    )(field, conv_w, spec_re, spec_im, mlp_in.T, mlp_out)
     return result.reshape(rows, depth, ch, width)
 
 

time: 108 us -> 107 us (level); the launches traced: 108 us -> 105 us
  Pallas kernels: 101 us -> 95.8 us
  local copies, waits for them, and re-layouts: 7.01 us -> 8.81 us
    pallas_call x1, Pallas kernels: 101 us -> 95.8 us  [per_device(): pl.pallas_call(functools.partial(kernel, n, m), out_shape=pltpu.VMEM((row...]
    unnamed x2 -> x13, local copies, waits for them, and re-layouts: 7.01 us -> 8.81 us
where the time goes in v1:
time: 107 us; the launch traced here: 105 us
  Pallas kernels  95.8 us (90%)
  local copies, waits for them, and re-layouts  8.81 us (8%)
    pallas_call x1, Pallas kernels, per_device(): pl.pallas_call(functools.partial(kernel, n, m), out_shape=pltpu.VMEM((row...  95.8 us
    unnamed x13, local copies, waits for them, and re-layouts  8.81 us

profile of v1, /device:TPU:1, one launch (start us, length us, event | category | flops | bytes accessed | tf_op | source)
XLA Modules:
  0.0 104.6 jit_solution(14906621979991235718)
XLA Ops:
  0.0 0.0 copy-start
  0.0 2.2 %copy-done = bf16[16,16,64,128]{3,2,1,0:T(8,128)(2,1)S(1)} copy-done((bf16[16,16,64,128]{3,2,1,0:T(8,128)(2,1)S(1)}, bf16[16,16,64,128]{3,2,1,0:T(8,128)(2,1)}, u32[]{:S(2)}) %copy-start) | copy-done | bytes 4194328
  2.2 0.0 copy-start.1
  2.2 1.0 copy-done.1
  3.2 0.0 copy-start.2
  3.2 1.0 copy-done.2
  4.3 0.0 copy-start.3
  4.3 1.0 copy-done.3
  5.3 0.0 copy-start.4
  5.3 0.8 copy-done.4
  6.0 0.0 copy-start.5
  6.0 0.8 copy-done.5
  6.8 95.8 %shard_map.64 = bf16[16,8,128,128]{3,2,1,0:T(8,128)(2,1)S(1)} custom-call(bf16[16,16,64,128]{3,2,1,0:T(8,128)(2,1)S(1)} %copy-done, bf16[27,64,64]{2,1,0:T(8,128)(2,1)S(1)} %copy-done.3, f32[16,64,64]{2,1,0:T(8,128)S(1)} %copy-done.1, f32[16,64,64]{2,1,0:T(8,128)S(1)} %copy-done.2, bf16[64,256]{1,0:T(8,128)(2,1)S(1)} %bitcast.3, bf16[64,256]{1,0:T(8,128)(2,1)S(1)} %copy-done.5), custom_call_target="tpu_custom_call" | custom-call | tf_op jit(solution)/shard_map/pallas_call | solution.py:362
  102.6 2.0 %copy.8 = bf16[16,16,64,128]{3,2,1,0:T(8,128)(2,1)} copy(bf16[16,16,64,128]{3,2,1,0:T(8,128)(2,1)S(1)} %bitcast.2) | data formatting | bytes 8388608
Async XLA Ops:
  0.0 2.2 %copy-start = (bf16[16,16,64,128]{3,2,1,0:T(8,128)(2,1)S(1)}, bf16[16,16,64,128]{3,2,1,0:T(8,128)(2,1)}, u32[]{:S(2)}) copy-start(bf16[16,16,64,128]{3,2,1,0:T(8,128)(2,1)} %field.1) | copy-start | bytes 12582916
  2.2 1.0 copy-start.1
  3.2 1.0 copy-start.2
  4.3 1.0 copy-start.3
  5.3 0.8 copy-start.4
  6.0 0.8 copy-start.5
